TPU v7x, 32 devices: a whole 2x2x4 slice. The times are simulated.
32 devices in a mesh: py: 8 (over y, x, core), pz: 4 (over z).
Axes of the slice: x: 2, y: 2, z: 4, core: 2. Of those that a mesh axis runs over, the one named last changes fastest.
Arguments:
- velocity: float32 [3, 32, 128, 2048], P(None, ('py', 'pz')), may hold values from -6 to 6
- fluid: float32 [32, 128, 2048], P(('py', 'pz')), may hold values from 0.1 to 1
- pressure: float32 [32, 128, 2048], P(None, 'pz', 'py'), may hold values from -4 to 4
Outputs:
- projected: float32 [3, 32, 128, 2048], P(None, ('py', 'pz'))
- divergence: float32 [32, 128, 2048], P(None, 'pz', 'py')
All inputs are finite; a program needn't handle non-finite values.
Results may differ from a plain program's by a relative error of at most 0.00002.
Values sent between devices are 32-bit elements; how exact they have to be, the bound alone decides.
A program may use at most 64 MiB of HBM per device.

v0:
```python
import jax
import jax.numpy as jnp
from jax import lax
from jax.sharding import PartitionSpec as P


def from_behind(shard, axis, by):
    size = lax.axis_size(axis)
    pairs = [(i, i + by) for i in range(size) if 0 <= i + by < size]
    return lax.ppermute(shard, axis, pairs)


def before_along(values, lower, axis):
    inner = lax.slice_in_dim(values, 0, values.shape[axis] - 1, axis=axis)
    return jnp.concatenate([lower, inner], axis)


def after_along(values, upper, axis):
    inner = lax.slice_in_dim(values, 1, values.shape[axis], axis=axis)
    return jnp.concatenate([inner, upper], axis)


def face_update(component, fluid, pressure, fluid_low, pressure_low, axis, first):
    index = lax.broadcasted_iota(jnp.int32, fluid.shape, axis) + first
    weight = jnp.where(
        index == 0, jnp.float32(0.0), 0.5 * (fluid + before_along(fluid, fluid_low, axis))
    )
    return weight * (component - (pressure - before_along(pressure, pressure_low, axis)))


def plane_zeros(values, axis):
    shape = list(values.shape)
    shape[axis] = 1
    return jnp.zeros(tuple(shape), jnp.float32)


def on_device(velocity, fluid, pressure):
    count_y = lax.axis_size("py")
    count_z = lax.axis_size("pz")
    x_dev = fluid.shape[0]
    depth = fluid.shape[1]
    across = fluid.shape[2]
    z_part = depth // count_z
    y_part = across // count_y
    pencil_x = pressure.shape[0]
    outgoing = pressure.reshape(count_y * count_z, pencil_x // (count_y * count_z), z_part, y_part)
    received = lax.all_to_all(outgoing, ("py", "pz"), split_axis=0, concat_axis=0, tiled=True)
    received = received.reshape(count_y, count_z, x_dev, z_part, y_part)
    slab_pressure = received.transpose(2, 1, 3, 0, 4).reshape(x_dev, depth, across)
    low_x = from_behind((fluid, slab_pressure), ("py", "pz"), 1)
    x_first = lax.axis_index(("py", "pz")) * x_dev
    z_zero = plane_zeros(fluid, 1)
    y_zero = plane_zeros(fluid, 2)
    along_x = face_update(velocity[0], fluid, slab_pressure, low_x[0], low_x[1], 0, x_first)
    along_z = face_update(velocity[1], fluid, slab_pressure, z_zero, z_zero, 1, 0)
    along_y = face_update(velocity[2], fluid, slab_pressure, y_zero, y_zero, 2, 0)
    high_x = from_behind(along_x, ("py", "pz"), -1)
    slab_div = after_along(along_x, high_x, 0) - along_x
    slab_div = slab_div + after_along(along_z, z_zero, 1) - along_z
    slab_div = slab_div + after_along(along_y, y_zero, 2) - along_y
    blocks = slab_div.reshape(x_dev, count_z, z_part, count_y, y_part)
    blocks = blocks.transpose(3, 1, 0, 2, 4).reshape(count_y * count_z, x_dev, z_part, y_part)
    arrived = lax.all_to_all(blocks, ("py", "pz"), split_axis=0, concat_axis=0, tiled=True)
    divergence = arrived.reshape(count_y * count_z * x_dev, z_part, y_part)
    projected = jnp.stack([along_x, along_z, along_y], 0)
    return (projected, divergence)


def solution(mesh):
    placed = (P(None, ("py", "pz"), None, None), P(("py", "pz"), None, None), P(None, "pz", "py"))
    return jax.shard_map(
        on_device,
        mesh=mesh,
        in_specs=placed,
        out_specs=(P(None, ("py", "pz"), None, None), P(None, "pz", "py")),
        check_vma=False,
    )
```

profile of v0, /device:TPU:1, one launch (start us, length us, event | category | flops | bytes accessed | tf_op | source)
XLA Modules:
  0.0 152.9 jit_solution(18236934584058507580)
XLA Ops:
  0.6 7.1 %all-to-all-start = ((f32[32,1,32,256]{3,2,1,0:T(8,128)}), f32[32,1,32,256]{3,2,1,0:T(8,128)S(1)}, u32[]{:S(2)}, u32[]{:S(2)}) async-start(f32[32,1,32,256]{3,2,1,0:T(8,128)} %bitcast.44), calls=%async_computation | async-start | bytes 2097152 | tf_op jit(solution)/shard_map/all_to_all | solution.py:47
  7.7 3.3 %collective-permute-start = (f32[1,128,2048]{2,1,0:T(8,128)}, f32[1,128,2048]{2,1,0:T(8,128)}, u32[]{:S(2)}, u32[]{:S(2)}) collective-permute-start(f32[1,128,2048]{2,1,0:T(8,128)} %param.4), channel_id=1, source_target_pairs={{0,1},{1,2},{2,3},{3,4},{4,5},{5,6},{6,7},{7,8},{8,9},{9,10},{10,1... | collective-permute-start | bytes 3145736 | tf_op jit(solution)/shard_map/ppermute | solution.py:10
  11.0 45.5 %all-to-all-done = f32[32,1,32,256]{3,2,1,0:T(8,128)S(1)} async-done(((f32[32,1,32,256]{3,2,1,0:T(8,128)}), f32[32,1,32,256]{3,2,1,0:T(8,128)S(1)}, u32[]{:S(2)}, u32[]{:S(2)}) %all-to-all-start) | async-done | bytes 1048608 | tf_op jit(solution)/shard_map/all_to_all | solution.py:47
  56.5 0.6 copy.7
  57.1 0.2 reshape.24
  57.3 1.9 %collective-permute-start.1 = (f32[1,128,2048]{2,1,0:T(8,128)S(1)}, f32[1,128,2048]{2,1,0:T(8,128)S(1)}, u32[]{:S(2)}, u32[]{:S(2)}) collective-permute-start(f32[1,128,2048]{2,1,0:T(8,128)S(1)} %reshape.24), channel_id=1, source_target_pairs={{0,1},{1,2},{2,3},{3,4},{4,5},{5,6},{6,7},{7,8},{8,9},{9,10},{10,1... | collective-permute-start | bytes 3145736 | tf_op jit(solution)/shard_map/ppermute | solution.py:10
  59.3 0.0 collective-permute-done
  59.3 26.3 %collective-permute-done.1 = f32[1,128,2048]{2,1,0:T(8,128)S(1)} collective-permute-done((f32[1,128,2048]{2,1,0:T(8,128)S(1)}, f32[1,128,2048]{2,1,0:T(8,128)S(1)}, u32[]{:S(2)}, u32[]{:S(2)}) %collective-permute-start.1) | collective-permute-done | bytes 1048608 | tf_op jit(solution)/shard_map/ppermute | solution.py:10
  85.5 1.0 copy-done.2
  86.5 4.8 %fusion.2 = (f32[1,128,2048]{2,1,0:T(8,128)S(1)}, f32[1,128,2048]{2,1,0:T(8,128)S(1)}, f32[1,128,2048]{2,1,0:T(8,128)S(1)}) fusion(f32[1,128,2048]{2,1,0:T(8,128)S(1)} %reshape.24, f32[1,128,2048]{2,1,0:T(8,128)} %copy-done.2, f32[3,1,128,2048]{3,2,1,0:T(8,128)} %param.3, f32[1,128,2048]{2,1,0:T(8,128)} %param.4, f32[1,128,2048]{2,1,0:T(8,128)} %collective-permute-done, ...), kind=kLoop, calls=%fused_computation.6 | loop fusion | flops 4718592 | bytes 14664833 | tf_op jit(solution)/shard_map/mul | solution.py:28
  91.3 0.0 copy-start
  91.3 1.9 %collective-permute-start.2 = (f32[1,128,2048]{2,1,0:T(8,128)S(1)}, f32[1,128,2048]{2,1,0:T(8,128)S(1)}, u32[]{:S(2)}, u32[]{:S(2)}) collective-permute-start(f32[1,128,2048]{2,1,0:T(8,128)S(1)} %get-tuple-element.2), channel_id=1, source_target_pairs={{1,0},{2,1},{3,2},{4,3},{5,4},{6,5},{7,6},{8,7},{9,8},{10,9},{11,1... | collective-permute-start | bytes 3145736 | tf_op jit(solution)/shard_map/ppermute | solution.py:10
  93.2 0.3 slice.39
  93.6 0.1 slice.38
  93.7 22.4 %collective-permute-done.2 = f32[1,128,2048]{2,1,0:T(8,128)S(1)} collective-permute-done((f32[1,128,2048]{2,1,0:T(8,128)S(1)}, f32[1,128,2048]{2,1,0:T(8,128)S(1)}, u32[]{:S(2)}, u32[]{:S(2)}) %collective-permute-start.2) | collective-permute-done | bytes 1048608 | tf_op jit(solution)/shard_map/ppermute | solution.py:10
  116.1 0.6 add_subtract_fusion
  116.7 0.0 copy-done
  116.7 0.0 copy-start.1
  116.7 0.3 copy.9
  117.1 1.3 copy.8
  118.4 5.8 %all-to-all-start.1 = ((f32[32,1,32,256]{3,2,1,0:T(8,128)}), f32[32,1,32,256]{3,2,1,0:T(8,128)}, u32[]{:S(2)}, u32[]{:S(2)}) async-start(f32[32,1,32,256]{3,2,1,0:T(8,128)} %bitcast.42), calls=%async_computation.1 | async-start | bytes 2097152 | tf_op jit(solution)/shard_map/all_to_all | solution.py:63
  124.2 1.9 %pad_maximum_fusion = f32[3,1,128,2048]{3,2,1,0:T(8,128)} fusion(f32[1,1,128,2048]{3,2,1,0:T(8,128)S(1)} %bitcast.33, f32[1,1,128,2048]{3,2,1,0:T(8,128)S(1)} %bitcast.34, f32[1,1,128,2048]{3,2,1,0:T(8,128)S(1)} %bitcast.37), kind=kLoop, calls=%fused_computation | loop fusion | flops 1572864 | bytes 6291456 | tf_op jit(solution)/shard_map/stack | solution.py:65
  126.1 24.5 %all-to-all-done.1 = f32[32,1,32,256]{3,2,1,0:T(8,128)} async-done(((f32[32,1,32,256]{3,2,1,0:T(8,128)}), f32[32,1,32,256]{3,2,1,0:T(8,128)}, u32[]{:S(2)}, u32[]{:S(2)}) %all-to-all-start.1) | async-done | bytes 1048608 | tf_op jit(solution)/shard_map/all_to_all | solution.py:63
  150.6 2.3 %copy.11 = f32[32,32,256]{2,1,0:T(8,128)} copy(f32[32,32,256]{2,1,0:T(8,128)} %bitcast.11) | data formatting | bytes 2097152
  (4 shorter events, 0.0 us)
Async XLA Ops:
  0.6 55.9 %all-to-all-start = ((f32[32,1,32,256]{3,2,1,0:T(8,128)}), f32[32,1,32,256]{3,2,1,0:T(8,128)S(1)}, u32[]{:S(2)}, u32[]{:S(2)}) async-start(f32[32,1,32,256]{3,2,1,0:T(8,128)} %bitcast.44), calls=%async_computation | async-start | bytes 2097152 | tf_op jit(solution)/shard_map/all_to_all | solution.py:47
  7.7 51.5 %collective-permute-start = (f32[1,128,2048]{2,1,0:T(8,128)}, f32[1,128,2048]{2,1,0:T(8,128)}, u32[]{:S(2)}, u32[]{:S(2)}) collective-permute-start(f32[1,128,2048]{2,1,0:T(8,128)} %param.4), channel_id=1, source_target_pairs={{0,1},{1,2},{2,3},{3,4},{4,5},{5,6},{6,7},{7,8},{8,9},{9,10},{10,1... | collective-permute-start | bytes 3145736 | tf_op jit(solution)/shard_map/ppermute | solution.py:10
  57.3 28.2 %collective-permute-start.1 = (f32[1,128,2048]{2,1,0:T(8,128)S(1)}, f32[1,128,2048]{2,1,0:T(8,128)S(1)}, u32[]{:S(2)}, u32[]{:S(2)}) collective-permute-start(f32[1,128,2048]{2,1,0:T(8,128)S(1)} %reshape.24), channel_id=1, source_target_pairs={{0,1},{1,2},{2,3},{3,4},{4,5},{5,6},{6,7},{7,8},{8,9},{9,10},{10,1... | collective-permute-start | bytes 3145736 | tf_op jit(solution)/shard_map/ppermute | solution.py:10
  85.5 1.0 copy-start.2
  91.3 25.4 %copy-start = (f32[1,128,2048]{2,1,0:T(8,128)}, f32[1,128,2048]{2,1,0:T(8,128)S(1)}, u32[]{:S(2)}) copy-start(f32[1,128,2048]{2,1,0:T(8,128)S(1)} %get-tuple-element.2) | copy-start | bytes 3145732
  91.3 24.8 %collective-permute-start.2 = (f32[1,128,2048]{2,1,0:T(8,128)S(1)}, f32[1,128,2048]{2,1,0:T(8,128)S(1)}, u32[]{:S(2)}, u32[]{:S(2)}) collective-permute-start(f32[1,128,2048]{2,1,0:T(8,128)S(1)} %get-tuple-element.2), channel_id=1, source_target_pairs={{1,0},{2,1},{3,2},{4,3},{5,4},{6,5},{7,6},{8,7},{9,8},{10,9},{11,1... | collective-permute-start | bytes 3145736 | tf_op jit(solution)/shard_map/ppermute | solution.py:10
  116.7 7.5 %copy-start.1 = (f32[1,128,2048]{2,1,0:T(8,128)S(1)}, f32[1,128,2048]{2,1,0:T(8,128)}, u32[]{:S(2)}) copy-start(f32[1,128,2048]{2,1,0:T(8,128)} %copy-done) | copy-start | bytes 3145732
  118.4 32.2 %all-to-all-start.1 = ((f32[32,1,32,256]{3,2,1,0:T(8,128)}), f32[32,1,32,256]{3,2,1,0:T(8,128)}, u32[]{:S(2)}, u32[]{:S(2)}) async-start(f32[32,1,32,256]{3,2,1,0:T(8,128)} %bitcast.42), calls=%async_computation.1 | async-start | bytes 2097152 | tf_op jit(solution)/shard_map/all_to_all | solution.py:63
where the time goes:
time: 153 us
  waiting for transfers between devices  119 us (78%)
  starting transfers between devices  20 us (13%)
  other arithmetic  7.29 us (5%)
  local copies, waits for them, and re-layouts  6.17 us (4%)
    ppermute x3, waiting for transfers between devices, from_behind(): return lax.ppermute(shard, axis, pairs)  48.7 us
    all_to_all x1, waiting for transfers between devices, on_device(): lax.all_to_all(outgoing, ('py', 'pz'), split_axis=0, concat_axis=0, tiled...  45.5 us
    all_to_all x1, waiting for transfers between devices, on_device(): lax.all_to_all(blocks, ('py', 'pz'), split_axis=0, concat_axis=0, tiled=T...  24.5 us
    ppermute x3, starting transfers between devices, from_behind(): return lax.ppermute(shard, axis, pairs)  7.11 us
    all_to_all x1, starting transfers between devices, on_device(): lax.all_to_all(outgoing, ('py', 'pz'), split_axis=0, concat_axis=0, tiled...  7.09 us
    all_to_all x1, starting transfers between devices, on_device(): lax.all_to_all(blocks, ('py', 'pz'), split_axis=0, concat_axis=0, tiled=T...  5.8 us
    mul x1, other arithmetic, face_update(): weight * (component - (pressure - before_along(pressure, pressure_low, ax...  4.78 us
    unnamed x8, local copies, waits for them, and re-layouts  3.63 us
  transfers between devices with their start and end apart: 5, of which 4 were waited for; matrix products, arithmetic and copies ran while one was open for 2% of the time, Pallas kernels for 0%

commit v1 on v0

v1 whole, which is shorter than its diff:
```python
import functools

import jax
import jax.numpy as jnp
from jax import lax
from jax.experimental import pallas as pl
from jax.experimental.pallas import tpu as pltpu
from jax.sharding import PartitionSpec as P

AHEAD = 2
LANES = 128


def kernel(
    count_y, count_z, v_hbm, f_hbm, p_hbm, out_hbm, div_hbm,
    v, f, f_low, main, halo, left, out, part, next_x, got, got_x, div,
    in_sem, put_sem,
    main_s, main_r, halo_s, halo_r, edge_s, edge_r, f_s, f_r, fwd_s, fwd_r, nx_s, nx_r,
    a_s, a_r, x_s, x_r,
):
    py = lax.axis_index("py")
    pz = lax.axis_index("pz")
    me = py * count_z + pz
    planes = count_y * count_z
    rows, across = f.shape
    width = across // count_y
    part_rows = rows // count_z
    half = count_z // 2 if count_z % 2 == 0 else 1
    half_rows = half * part_rows

    def side(z):
        return z // half if isinstance(z, int) else lax.div(z, half)

    def joined(z):
        return min((z + 1) % half, 1) if isinstance(z, int) else jnp.minimum(lax.rem(z + 1, half), 1)

    def cols(c):
        return pl.ds(pl.multiple_of(c * width, width), width)

    def band(g):
        return pl.ds(g * part_rows, part_rows)

    other = pl.ds(pl.multiple_of(jnp.where(side(pz) == 0, rows - half_rows, 0), part_rows), half_rows)

    def wrap(c):
        return lax.rem(c + 2 * count_y, count_y)

    def remote(src, dst, send, recv, y, z):
        return pltpu.make_async_remote_copy(
            src_ref=src, dst_ref=dst, send_sem=send, recv_sem=recv,
            device_id=(y, z), device_id_type=pl.DeviceIdType.MESH,
        )

    def begin(src, dst, send, recv, y, z, gate=1, away=False):
        apart = 1 if away else jnp.abs(y * count_z + z - me)

        @pl.when(jnp.minimum(gate, apart) > 0)
        def _():
            remote(src, dst, send, recv, y, z).start()

        if not away:
            @pl.when(gate - jnp.minimum(apart, 1) > 0)
            def _():
                pltpu.make_async_copy(src, dst, recv).start()

    def sent(src, dst, send, recv, y, z, gate=1, away=False):
        apart = 1 if away else jnp.abs(y * count_z + z - me)

        @pl.when(jnp.minimum(gate, apart) > 0)
        def _():
            remote(src, dst, send, recv, y, z).wait_send()

    def landed(dst, recv):
        pltpu.make_async_copy(dst, dst, recv).wait()

    def direct(z, g):
        return 1 - joined(z - 1) * jnp.minimum(jnp.abs(side(g) - side(z)), 1)

    loads = [
        pltpu.make_async_copy(v_hbm.at[:, 0], v, in_sem.at[0]),
        pltpu.make_async_copy(f_hbm.at[0], f, in_sem.at[1]),
    ]
    for load in loads:
        load.start()

    barrier = pltpu.get_barrier_semaphore()

    def greet(i, carry):
        @pl.when(i != me)
        def _():
            pl.semaphore_signal(
                barrier, inc=1, device_id=(lax.div(i, count_z), lax.rem(i, count_z)),
                device_id_type=pl.DeviceIdType.MESH,
            )
        return carry

    lax.fori_loop(0, planes, greet, 0)
    pl.semaphore_wait(barrier, planes - 1)

    mine = pl.ds(pl.multiple_of(pz * part_rows, part_rows), part_rows)
    ahead_y = lax.div(me + 1, count_z)
    ahead_z = lax.rem(me + 1, count_z)

    def pressure_sends(k, do):
        y = wrap(py - k)
        for z in range(count_z):
            target = y * count_z + z
            slot = k * count_z + z
            do(p_hbm.at[target], main.at[mine, cols(py)], main_s.at[slot], main_r.at[k * count_z + pz], y, z)

            do(p_hbm.at[jnp.maximum(target - 1, 0)], halo.at[mine, cols(py)],
               halo_s.at[slot], halo_r.at[k * count_z + pz], y, z, gate=direct(z, pz))
        c = cols(wrap(ahead_y + k))
        do(f_hbm.at[0, :, c], f_low.at[:, c], f_s.at[k], f_r.at[k], ahead_y, ahead_z,
           gate=planes - 1 - me, away=True)

    def edge_sends(do):
        for z in range(count_z):
            y = wrap(py + 1)
            do(p_hbm.at[y * count_z + z, :, width - LANES:], left.at[mine],
               edge_s.at[z], edge_r.at[pz], y, z, away=True)

    def forward(k, do):
        c = cols(wrap(py + k))
        do(main.at[other, c], halo.at[other, c], fwd_s.at[k], fwd_r.at[k], py, pz + 1,
           gate=joined(pz), away=True)

    def lend(k, do):
        c = cols(wrap(py + k))
        do(out.at[0, other, c], next_x.at[:, c], nx_s.at[k], nx_r.at[k], py, pz - 1,
           gate=joined(pz - 1), away=True)

    def result_sends(k, do):
        y = wrap(py + k)
        for z in range(count_z):
            slot = k * count_z + z
            do(part.at[band(z), cols(y)], got.at[me], a_s.at[slot], a_r.at[me], y, z)
            below = jnp.maximum(me - 1, 0)
            do(out.at[0, band(z), cols(y)], got_x.at[below], x_s.at[slot], x_r.at[below], y, z,
               gate=jnp.minimum(me, direct(pz, z)))

    edge_sends(begin)
    for k in range(min(AHEAD, count_y)):
        pressure_sends(k, begin)
    for load in loads:
        load.wait()
    for z in range(count_z):
        landed(left.at[band(z)], edge_r.at[z])

    def before(tile, values):
        wide = jnp.concatenate([tile, values], 1)
        return pltpu.roll(wide, 1, 1)[:, LANES:]

    def project(k):
        @pl.when(k + AHEAD < count_y)
        def _():
            pressure_sends(k + AHEAD, begin)

        y = wrap(py + k)
        c = cols(y)
        for z in range(count_z):
            landed(main.at[band(z), c], main_r.at[k * count_z + z])
        forward(k, begin)
        for z in range(count_z):
            @pl.when(direct(pz, z) > 0)
            def _():
                landed(halo.at[band(z), c], halo_r.at[k * count_z + z])

        @pl.when(joined(pz - 1) > 0)
        def _():
            landed(halo.at[other, c], fwd_r.at[k])

        @pl.when(me > 0)
        def _():
            landed(f_low.at[:, c], f_r.at[k])

        fluid = f[:, c]
        here = main[:, c]
        w_x = 0.5 * (fluid + f_low[:, c])
        along_x = w_x * (v[0, :, c] - (here - halo[:, c]))
        out[0, :, c] = jnp.where(me == 0, jnp.float32(0.0), along_x)
        lend(k, begin)
        z_index = lax.broadcasted_iota(jnp.int32, fluid.shape, 0)
        w_z = 0.5 * (fluid + pltpu.roll(fluid, 1, 0))
        along_z = w_z * (v[1, :, c] - (here - pltpu.roll(here, 1, 0)))
        out[1, :, c] = jnp.where(z_index == 0, jnp.float32(0.0), along_z)
        y_index = lax.broadcasted_iota(jnp.int32, fluid.shape, 1) + y * width
        f_tile = f[:, pl.ds(pl.multiple_of(wrap(y - 1) * width + (width - LANES), LANES), LANES)]
        w_y = 0.5 * (fluid + before(f_tile, fluid))
        along_y = w_y * (v[2, :, c] - (here - before(left[...], here)))
        out[2, :, c] = jnp.where(y_index == 0, jnp.float32(0.0), along_y)
        left[...] = here[:, width - LANES:]
        pltpu.make_async_copy(out.at[:, :, c], out_hbm.at[:, 0, :, c], put_sem.at[k]).start()

    def diverge(k):
        y = wrap(py + k)
        c = cols(y)
        along_z = out[1, :, c]
        along_y = out[2, :, c]
        z_index = lax.broadcasted_iota(jnp.int32, along_z.shape, 0)
        y_index = lax.broadcasted_iota(jnp.int32, along_z.shape, 1) + y * width
        z_next = jnp.where(z_index == rows - 1, jnp.float32(0.0), pltpu.roll(along_z, rows - 1, 0))
        tile = out[2, :, pl.ds(pl.multiple_of(wrap(y + 1) * width, width), LANES)]
        wide = pltpu.roll(jnp.concatenate([along_y, tile], 1), width + LANES - 1, 1)[:, :width]
        y_next = jnp.where(y_index == across - 1, jnp.float32(0.0), wide)
        part[:, c] = (z_next - along_z) + (y_next - along_y) - out[0, :, c]

        @pl.when(joined(pz) > 0)
        def _():
            landed(next_x.at[:, c], nx_r.at[k])
            part[other, c] = part[other, c] + next_x[:, c]

        result_sends(k, begin)

    def step(k, carry):
        @pl.when(k < count_y)
        def _():
            project(k)

        @pl.when(k > 0)
        def _():
            diverge(k - 1)
        return carry

    lax.fori_loop(0, count_y + 1, step, 0)

    def collect(i, carry):
        y = wrap(py - i - 1)
        for z in range(count_z):
            q = y * count_z + z
            landed(got.at[q], a_r.at[q])
            added = jnp.minimum(planes - 1 - q, 1 - joined(z) * jnp.abs(side(pz) - side(z)))

            @pl.when(added > 0)
            def _():
                landed(got_x.at[q], x_r.at[q])
                div[q] = got[q] + got_x[q]

            @pl.when(added <= 0)
            def _():
                div[q] = got[q]
        group = pl.ds(y * count_z, count_z)
        pltpu.make_async_copy(div.at[group], div_hbm.at[group], put_sem.at[count_y + i]).start()
        return carry

    lax.fori_loop(0, count_y, collect, 0)

    def finish(k, carry):
        pressure_sends(k, sent)
        forward(k, sent)
        lend(k, sent)
        result_sends(k, sent)
        c = cols(wrap(py + k))
        pltpu.make_async_copy(out.at[:, :, c], out_hbm.at[:, 0, :, c], put_sem.at[k]).wait()
        group = pl.ds(wrap(py - k - 1) * count_z, count_z)
        pltpu.make_async_copy(div.at[group], div_hbm.at[group], put_sem.at[count_y + k]).wait()
        return carry

    edge_sends(sent)
    lax.fori_loop(0, count_y, finish, 0)


def on_device(velocity, fluid, pressure):
    count_y = lax.axis_size("py")
    count_z = lax.axis_size("pz")
    rows, across = fluid.shape[1:]
    planes = pressure.shape[0]
    block = pressure.shape[1:]
    half_rows = (count_z // 2 if count_z % 2 == 0 else 1) * (rows // count_z)
    vm = lambda *shape: pltpu.VMEM(shape, jnp.float32)
    dma = lambda n: pltpu.SemaphoreType.DMA((n,))
    steps = count_y * count_z
    return pl.pallas_call(
        functools.partial(kernel, count_y, count_z),
        out_shape=(
            jax.ShapeDtypeStruct(velocity.shape, jnp.float32),
            jax.ShapeDtypeStruct(pressure.shape, jnp.float32),
        ),
        in_specs=[pl.BlockSpec(memory_space=pl.ANY)] * 3,
        out_specs=(pl.BlockSpec(memory_space=pl.ANY),) * 2,
        scratch_shapes=[
            vm(3, rows, across), vm(rows, across), vm(rows, across), vm(rows, across), vm(rows, across),
            vm(rows, LANES), vm(3, rows, across), vm(rows, across), vm(half_rows, across),
            vm(planes, *block), vm(planes, *block), vm(planes, *block),
            dma(2), dma(2 * count_y),
            dma(steps), dma(steps), dma(steps), dma(steps), dma(count_z), dma(count_z),
            dma(count_y), dma(count_y), dma(count_y), dma(count_y), dma(count_y), dma(count_y),
            dma(steps), dma(planes), dma(steps), dma(planes),
        ],
        compiler_params=pltpu.CompilerParams(
            collective_id=0, has_side_effects=True, vmem_limit_bytes=40 << 20
        ),
        name="project_all",
    )(velocity, fluid, pressure)


def solution(mesh):
    placed = (P(None, ("py", "pz"), None, None), P(("py", "pz"), None, None), P(None, "pz", "py"))
    return jax.shard_map(
        on_device,
        mesh=mesh,
        in_specs=placed,
        out_specs=(P(None, ("py", "pz"), None, None), P(None, "pz", "py")),
        check_vma=False,
    )
```

time: 153 us -> 123 us (0.80)
  waiting for transfers between devices: 119 us -> 0 us
  Pallas kernels: 0 us -> 114 us
  starting transfers between devices: 20 us -> 0 us
  other arithmetic: 7.29 us -> 0 us
    pallas_call x0 -> x1, Pallas kernels: none -> 114 us  [on_device(): pl.pallas_call(functools.partial(kernel, count_y, count_z), out_shape=(ja...]
    all_to_all x2 -> x0, waiting for transfers between devices: 70 us -> none  [the longest x1 45.5 us: on_device(): lax.all_to_all(outgoing, ('py', 'pz'), split_axis=0, concat_axis=0, tiled...]
    ppermute x3 -> x0, waiting for transfers between devices: 48.7 us -> none  [from_behind(): return lax.ppermute(shard, axis, pairs)]
    all_to_all x2 -> x0, starting transfers between devices: 12.9 us -> none  [the longest x1 7.09 us: on_device(): lax.all_to_all(outgoing, ('py', 'pz'), split_axis=0, concat_axis=0, tiled...]
    ppermute x3 -> x0, starting transfers between devices: 7.11 us -> none  [from_behind(): return lax.ppermute(shard, axis, pairs)]
    mul x1 -> x0, other arithmetic: 4.78 us -> none  [face_update(): weight * (component - (pressure - before_along(pressure, pressure_low, ax...]
    unnamed x8, local copies, waits for them, and re-layouts: 3.63 us -> 6.97 us
    another operation x1 -> x0, other arithmetic: 1.87 us -> none  [on_device(): projected = jnp.stack([along_x, along_z, along_y], 0)]
  transfers between devices with their start and end apart: 5 -> 0, of which waited for: 4 -> 0; matrix products, arithmetic and copies ran while one was open for 2% -> 0% of each run, Pallas kernels for 0% -> 0%
where the time goes in v1:
time: 123 us; the launch traced here: 122 us
  Pallas kernels  114 us (93%)
  local copies, waits for them, and re-layouts  6.97 us (6%)
    pallas_call x1, Pallas kernels, on_device(): pl.pallas_call(functools.partial(kernel, count_y, count_z), out_shape=(ja...  114 us
    unnamed x8, local copies, waits for them, and re-layouts  6.97 us

profile of v1, /device:TPU:1, one launch (start us, length us, event | category | flops | bytes accessed | tf_op | source)
XLA Modules:
  0.0 121.6 jit_solution(12733781687853393007)
XLA Ops:
  0.6 0.0 copy-start
  0.6 1.9 %copy-done = f32[3,1,128,2048]{3,2,1,0:T(8,128)S(1)} copy-done((f32[3,1,128,2048]{3,2,1,0:T(8,128)S(1)}, f32[3,1,128,2048]{3,2,1,0:T(8,128)}, u32[]{:S(2)}) %copy-start) | copy-done | bytes 3145752
  2.5 0.0 copy-start.1
  2.5 1.2 %copy-done.1 = f32[1,128,2048]{2,1,0:T(8,128)S(1)} copy-done((f32[1,128,2048]{2,1,0:T(8,128)S(1)}, f32[1,128,2048]{2,1,0:T(8,128)}, u32[]{:S(2)}) %copy-start.1) | copy-done | bytes 1048600
  3.7 0.0 copy-start.2
  3.7 1.2 %copy-done.2 = f32[32,32,256]{2,1,0:T(8,128)S(1)} copy-done((f32[32,32,256]{2,1,0:T(8,128)S(1)}, f32[32,32,256]{2,1,0:T(8,128)}, u32[]{:S(2)}) %copy-start.2) | copy-done | bytes 1048600
  5.0 114.0 %project_all.1 = (f32[3,1,128,2048]{3,2,1,0:T(8,128)S(1)}, f32[32,32,256]{2,1,0:T(8,128)S(1)}) custom-call(f32[3,1,128,2048]{3,2,1,0:T(8,128)S(1)} %copy-done, f32[1,128,2048]{2,1,0:T(8,128)S(1)} %copy-done.1, f32[32,32,256]{2,1,0:T(8,128)S(1)} %copy-done.2), custom_call_target="tpu_custom_call" | custom-call | tf_op jit(solution)/shard_map/project_all/pallas_call | solution.py:273
  118.9 1.7 %copy.7 = f32[3,1,128,2048]{3,2,1,0:T(8,128)} copy(f32[3,1,128,2048]{3,2,1,0:T(8,128)S(1)} %get-tuple-element.4) | data formatting | bytes 6291456
  120.6 1.0 copy.8
Async XLA Ops:
  0.6 1.9 %copy-start = (f32[3,1,128,2048]{3,2,1,0:T(8,128)S(1)}, f32[3,1,128,2048]{3,2,1,0:T(8,128)}, u32[]{:S(2)}) copy-start(f32[3,1,128,2048]{3,2,1,0:T(8,128)} %v_hbm.1) | copy-start | bytes 9437188
  2.5 1.2 %copy-start.1 = (f32[1,128,2048]{2,1,0:T(8,128)S(1)}, f32[1,128,2048]{2,1,0:T(8,128)}, u32[]{:S(2)}) copy-start(f32[1,128,2048]{2,1,0:T(8,128)} %f_hbm.1) | copy-start | bytes 3145732
  3.7 1.2 %copy-start.2 = (f32[32,32,256]{2,1,0:T(8,128)S(1)}, f32[32,32,256]{2,1,0:T(8,128)}, u32[]{:S(2)}) copy-start(f32[32,32,256]{2,1,0:T(8,128)} %p_hbm.1) | copy-start | bytes 3145732

commit v2 on v1

--- a/solution.py
+++ b/solution.py
@@ -12,8 +12,8 @@
 
 
 def kernel(
-    count_y, count_z, v_hbm, f_hbm, p_hbm, out_hbm, div_hbm,
-    v, f, f_low, main, halo, left, out, part, next_x, got, got_x, div,
+    count_y, count_z, v_hbm, f_hbm, p_hbm, out_hbm, div,
+    v, f, f_low, main, halo, left, out, part, next_x, got, got_x,
     in_sem, put_sem,
     main_s, main_r, halo_s, halo_r, edge_s, edge_r, f_s, f_r, fwd_s, fwd_r, nx_s, nx_r,
     a_s, a_r, x_s, x_r,
@@ -26,7 +26,6 @@
     width = across // count_y
     part_rows = rows // count_z
     half = count_z // 2 if count_z % 2 == 0 else 1
-    half_rows = half * part_rows
 
     def side(z):
         return z // half if isinstance(z, int) else lax.div(z, half)
@@ -39,8 +38,6 @@
 
     def band(g):
         return pl.ds(g * part_rows, part_rows)
-
-    other = pl.ds(pl.multiple_of(jnp.where(side(pz) == 0, rows - half_rows, 0), part_rows), half_rows)
 
     def wrap(c):
         return lax.rem(c + 2 * count_y, count_y)
@@ -73,8 +70,15 @@
     def landed(dst, recv):
         pltpu.make_async_copy(dst, dst, recv).wait()
 
-    def direct(z, g):
-        return 1 - joined(z - 1) * jnp.minimum(jnp.abs(side(g) - side(z)), 1)
+    def passed(z, g):
+        low, high = (min, max) if isinstance(z, int) and isinstance(g, int) else (jnp.minimum, jnp.maximum)
+        apart = low(high(abs(g - z) - 1, 0), 1)
+        across_middle = joined(z - 1) * low(abs(side(g) - side(z)), 1)
+        return low(high(apart, across_middle), low(z, 1))
+
+    def passed_up(z, g):
+        return passed(z + 1, g) if isinstance(z, int) and z < count_z - 1 else (
+            0 if isinstance(z, int) else jnp.minimum(passed(z + 1, g), count_z - 1 - z))
 
     loads = [
         pltpu.make_async_copy(v_hbm.at[:, 0], v, in_sem.at[0]),
@@ -109,7 +113,7 @@
             do(p_hbm.at[target], main.at[mine, cols(py)], main_s.at[slot], main_r.at[k * count_z + pz], y, z)
 
             do(p_hbm.at[jnp.maximum(target - 1, 0)], halo.at[mine, cols(py)],
-               halo_s.at[slot], halo_r.at[k * count_z + pz], y, z, gate=direct(z, pz))
+               halo_s.at[slot], halo_r.at[k * count_z + pz], y, z, gate=1 - passed(z, pz))
         c = cols(wrap(ahead_y + k))
         do(f_hbm.at[0, :, c], f_low.at[:, c], f_s.at[k], f_r.at[k], ahead_y, ahead_z,
            gate=planes - 1 - me, away=True)
@@ -122,13 +126,17 @@
 
     def forward(k, do):
         c = cols(wrap(py + k))
-        do(main.at[other, c], halo.at[other, c], fwd_s.at[k], fwd_r.at[k], py, pz + 1,
-           gate=joined(pz), away=True)
+        for g in range(count_z):
+            slot = k * count_z + g
+            do(main.at[band(g), c], halo.at[band(g), c], fwd_s.at[slot], fwd_r.at[slot], py, pz + 1,
+               gate=passed_up(pz, g), away=True)
 
     def lend(k, do):
         c = cols(wrap(py + k))
-        do(out.at[0, other, c], next_x.at[:, c], nx_s.at[k], nx_r.at[k], py, pz - 1,
-           gate=joined(pz - 1), away=True)
+        for g in range(count_z):
+            slot = k * count_z + g
+            do(out.at[0, band(g), c], next_x.at[band(g), c], nx_s.at[slot], nx_r.at[slot], py, pz - 1,
+               gate=passed(pz, g), away=True)
 
     def result_sends(k, do):
         y = wrap(py + k)
@@ -137,7 +145,7 @@
             do(part.at[band(z), cols(y)], got.at[me], a_s.at[slot], a_r.at[me], y, z)
             below = jnp.maximum(me - 1, 0)
             do(out.at[0, band(z), cols(y)], got_x.at[below], x_s.at[slot], x_r.at[below], y, z,
-               gate=jnp.minimum(me, direct(pz, z)))
+               gate=jnp.minimum(me, 1 - passed(pz, z)))
 
     edge_sends(begin)
     for k in range(min(AHEAD, count_y)):
@@ -162,13 +170,13 @@
             landed(main.at[band(z), c], main_r.at[k * count_z + z])
         forward(k, begin)
         for z in range(count_z):
-            @pl.when(direct(pz, z) > 0)
+            @pl.when(passed(pz, z) == 0)
             def _():
                 landed(halo.at[band(z), c], halo_r.at[k * count_z + z])
 
-        @pl.when(joined(pz - 1) > 0)
-        def _():
-            landed(halo.at[other, c], fwd_r.at[k])
+            @pl.when(passed(pz, z) > 0)
+            def _():
+                landed(halo.at[band(z), c], fwd_r.at[k * count_z + z])
 
         @pl.when(me > 0)
         def _():
@@ -205,10 +213,11 @@
         y_next = jnp.where(y_index == across - 1, jnp.float32(0.0), wide)
         part[:, c] = (z_next - along_z) + (y_next - along_y) - out[0, :, c]
 
-        @pl.when(joined(pz) > 0)
-        def _():
-            landed(next_x.at[:, c], nx_r.at[k])
-            part[other, c] = part[other, c] + next_x[:, c]
+        for g in range(count_z):
+            @pl.when(passed_up(pz, g) > 0)
+            def _():
+                landed(next_x.at[band(g), c], nx_r.at[k * count_z + g])
+                part[band(g), c] = part[band(g), c] + next_x[band(g), c]
 
         result_sends(k, begin)
 
@@ -229,7 +238,7 @@
         for z in range(count_z):
             q = y * count_z + z
             landed(got.at[q], a_r.at[q])
-            added = jnp.minimum(planes - 1 - q, 1 - joined(z) * jnp.abs(side(pz) - side(z)))
+            added = jnp.minimum(planes - 1 - q, 1 - passed_up(z, pz))
 
             @pl.when(added > 0)
             def _():
@@ -239,8 +248,6 @@
             @pl.when(added <= 0)
             def _():
                 div[q] = got[q]
-        group = pl.ds(y * count_z, count_z)
-        pltpu.make_async_copy(div.at[group], div_hbm.at[group], put_sem.at[count_y + i]).start()
         return carry
 
     lax.fori_loop(0, count_y, collect, 0)
@@ -252,8 +259,6 @@
         result_sends(k, sent)
         c = cols(wrap(py + k))
         pltpu.make_async_copy(out.at[:, :, c], out_hbm.at[:, 0, :, c], put_sem.at[k]).wait()
-        group = pl.ds(wrap(py - k - 1) * count_z, count_z)
-        pltpu.make_async_copy(div.at[group], div_hbm.at[group], put_sem.at[count_y + k]).wait()
         return carry
 
     edge_sends(sent)
@@ -266,7 +271,6 @@
     rows, across = fluid.shape[1:]
     planes = pressure.shape[0]
     block = pressure.shape[1:]
-    half_rows = (count_z // 2 if count_z % 2 == 0 else 1) * (rows // count_z)
     vm = lambda *shape: pltpu.VMEM(shape, jnp.float32)
     dma = lambda n: pltpu.SemaphoreType.DMA((n,))
     steps = count_y * count_z
@@ -276,19 +280,18 @@
             jax.ShapeDtypeStruct(velocity.shape, jnp.float32),
             jax.ShapeDtypeStruct(pressure.shape, jnp.float32),
         ),
-        in_specs=[pl.BlockSpec(memory_space=pl.ANY)] * 3,
-        out_specs=(pl.BlockSpec(memory_space=pl.ANY),) * 2,
+        in_specs=[pl.BlockSpec(memory_space=pltpu.MemorySpace.HBM)] * 3,
+        out_specs=(pl.BlockSpec(memory_space=pl.ANY), pl.BlockSpec(memory_space=pltpu.VMEM)),
         scratch_shapes=[
             vm(3, rows, across), vm(rows, across), vm(rows, across), vm(rows, across), vm(rows, across),
-            vm(rows, LANES), vm(3, rows, across), vm(rows, across), vm(half_rows, across),
-            vm(planes, *block), vm(planes, *block), vm(planes, *block),
-            dma(2), dma(2 * count_y),
+            vm(rows, LANES), vm(3, rows, across), vm(rows, across), vm(rows, across),
+            vm(planes, *block), vm(planes, *block), dma(2), dma(count_y),
             dma(steps), dma(steps), dma(steps), dma(steps), dma(count_z), dma(count_z),
-            dma(count_y), dma(count_y), dma(count_y), dma(count_y), dma(count_y), dma(count_y),
+            dma(count_y), dma(count_y), dma(steps), dma(steps), dma(steps), dma(steps),
             dma(steps), dma(planes), dma(steps), dma(planes),
         ],
         compiler_params=pltpu.CompilerParams(
-            collective_id=0, has_side_effects=True, vmem_limit_bytes=40 << 20
+            collective_id=0, has_side_effects=True, vmem_limit_bytes=52 << 20
         ),
         name="project_all",
     )(velocity, fluid, pressure)

time: 123 us -> 113 us (0.919); the launches traced: 122 us -> 113 us
  Pallas kernels: 114 us -> 108 us
  local copies, waits for them, and re-layouts: 6.97 us -> 4.88 us
    pallas_call x1, Pallas kernels: 114 us -> 108 us  [on_device(): pl.pallas_call(functools.partial(kernel, count_y, count_z), out_shape=(ja...]
    unnamed x8 -> x2, local copies, waits for them, and re-layouts: 6.97 us -> 4.88 us
where the time goes in v2:
time: 113 us
  Pallas kernels  108 us (96%)
  local copies, waits for them, and re-layouts  4.88 us (4%)
    pallas_call x1, Pallas kernels, on_device(): pl.pallas_call(functools.partial(kernel, count_y, count_z), out_shape=(ja...  108 us
    unnamed x2, local copies, waits for them, and re-layouts  4.88 us

profile of v2, /device:TPU:1, one launch (start us, length us, event | category | flops | bytes accessed | tf_op | source)
XLA Modules:
  0.0 113.1 jit_solution(3203204214419808340)
XLA Ops:
  0.6 107.6 %project_all.1 = (f32[3,1,128,2048]{3,2,1,0:T(8,128)}, f32[32,32,256]{2,1,0:T(8,128)S(1)}) custom-call(f32[3,1,128,2048]{3,2,1,0:T(8,128)} %v_hbm.1, f32[1,128,2048]{2,1,0:T(8,128)} %f_hbm.1, f32[32,32,256]{2,1,0:T(8,128)} %p_hbm.1), custom_call_target="tpu_custom_call" | custom-call | tf_op jit(solution)/shard_map/project_all/pallas_call | solution.py:277
  108.2 3.9 %copy.7 = f32[3,1,128,2048]{3,2,1,0:T(8,128)} copy(f32[3,1,128,2048]{3,2,1,0:T(8,128)} %get-tuple-element.4) | data formatting | bytes 6291456
  112.1 1.0 copy.8

commit v3 on v2

--- a/solution.py
+++ b/solution.py
@@ -12,12 +12,13 @@
 
 
 def kernel(
-    count_y, count_z, v_hbm, f_hbm, p_hbm, out_hbm, div,
-    v, f, f_low, main, halo, left, out, part, next_x, got, got_x,
-    in_sem, put_sem,
+    count_y, count_z, v_hbm, f_hbm, p_hbm, out_ref, div,
+    v, f, f_low, main, halo, left, part, next_x, got, got_x,
+    in_sem,
     main_s, main_r, halo_s, halo_r, edge_s, edge_r, f_s, f_r, fwd_s, fwd_r, nx_s, nx_r,
     a_s, a_r, x_s, x_r,
 ):
+    out = out_ref.at[:, 0]
     py = lax.axis_index("py")
     pz = lax.axis_index("pz")
     me = py * count_z + pz
@@ -198,7 +199,6 @@
         along_y = w_y * (v[2, :, c] - (here - before(left[...], here)))
         out[2, :, c] = jnp.where(y_index == 0, jnp.float32(0.0), along_y)
         left[...] = here[:, width - LANES:]
-        pltpu.make_async_copy(out.at[:, :, c], out_hbm.at[:, 0, :, c], put_sem.at[k]).start()
 
     def diverge(k):
         y = wrap(py + k)
@@ -257,8 +257,6 @@
         forward(k, sent)
         lend(k, sent)
         result_sends(k, sent)
-        c = cols(wrap(py + k))
-        pltpu.make_async_copy(out.at[:, :, c], out_hbm.at[:, 0, :, c], put_sem.at[k]).wait()
         return carry
 
     edge_sends(sent)
@@ -281,20 +279,20 @@
             jax.ShapeDtypeStruct(pressure.shape, jnp.float32),
         ),
         in_specs=[pl.BlockSpec(memory_space=pltpu.MemorySpace.HBM)] * 3,
-        out_specs=(pl.BlockSpec(memory_space=pl.ANY), pl.BlockSpec(memory_space=pltpu.VMEM)),
+        out_specs=(pl.BlockSpec(memory_space=pltpu.VMEM),) * 2,
         scratch_shapes=[
             vm(3, rows, across), vm(rows, across), vm(rows, across), vm(rows, across), vm(rows, across),
-            vm(rows, LANES), vm(3, rows, across), vm(rows, across), vm(rows, across),
-            vm(planes, *block), vm(planes, *block), dma(2), dma(count_y),
+            vm(rows, LANES), vm(rows, across), vm(rows, across),
+            vm(planes, *block), vm(planes, *block), dma(2),
             dma(steps), dma(steps), dma(steps), dma(steps), dma(count_z), dma(count_z),
             dma(count_y), dma(count_y), dma(steps), dma(steps), dma(steps), dma(steps),
             dma(steps), dma(planes), dma(steps), dma(planes),
         ],
         compiler_params=pltpu.CompilerParams(
-            collective_id=0, has_side_effects=True, vmem_limit_bytes=52 << 20
+            collective_id=0, has_side_effects=True, vmem_limit_bytes=40 << 20
         ),
         name="project_all",
-    )(velocity, fluid, pressure)
+    )(*(pltpu.with_memory_space_constraint(x, pltpu.MemorySpace.HBM) for x in (velocity, fluid, pressure)))
 
 
 def solution(mesh):

time: 113 us -> 111 us (0.982)
  local copies, waits for them, and re-layouts: 4.88 us -> 2.64 us
    unnamed x2, local copies, waits for them, and re-layouts: 4.88 us -> 2.64 us
where the time goes in v3:
time: 111 us
  Pallas kernels  107 us (96%)
  local copies, waits for them, and re-layouts  2.64 us (2%)
    pallas_call x1, Pallas kernels, on_device(): pl.pallas_call(functools.partial(kernel, count_y, count_z), out_shape=(ja...  107 us
    unnamed x2, local copies, waits for them, and re-layouts  2.64 us

profile of v3, /device:TPU:1, one launch (start us, length us, event | category | flops | bytes accessed | tf_op | source)
XLA Modules:
  0.0 110.7 jit_solution(5005462510228358267)
XLA Ops:
  0.6 107.5 %project_all.1 = (f32[3,1,128,2048]{3,2,1,0:T(8,128)S(1)}, f32[32,32,256]{2,1,0:T(8,128)S(1)}) custom-call(f32[3,1,128,2048]{3,2,1,0:T(8,128)} %v_hbm.1, f32[1,128,2048]{2,1,0:T(8,128)} %f_hbm.1, f32[32,32,256]{2,1,0:T(8,128)} %p_hbm.1), custom_call_target="tpu_custom_call" | custom-call | tf_op jit(solution)/shard_map/project_all/pallas_call | solution.py:275
  108.1 1.7 %copy.7 = f32[3,1,128,2048]{3,2,1,0:T(8,128)} copy(f32[3,1,128,2048]{3,2,1,0:T(8,128)S(1)} %get-tuple-element.4) | data formatting | bytes 6291456
  109.8 1.0 copy.8

commit v4 on v3

--- a/solution.py
+++ b/solution.py
@@ -13,7 +13,7 @@
 
 def kernel(
     count_y, count_z, v_hbm, f_hbm, p_hbm, out_ref, div,
-    v, f, f_low, main, halo, left, part, next_x, got, got_x,
+    v, f, f_low, main, halo, left, tail, packed, edge, part, next_x, got, got_x,
     in_sem,
     main_s, main_r, halo_s, halo_r, edge_s, edge_r, f_s, f_r, fwd_s, fwd_r, nx_s, nx_r,
     a_s, a_r, x_s, x_r,
@@ -85,8 +85,18 @@
         pltpu.make_async_copy(v_hbm.at[:, 0], v, in_sem.at[0]),
         pltpu.make_async_copy(f_hbm.at[0], f, in_sem.at[1]),
     ]
+    next_line = pl.ds(wrap(py + 1) * count_z, count_z)
+    loads.append(pltpu.make_async_copy(p_hbm.at[next_line, :, width - LANES:], tail, in_sem.at[2]))
     for load in loads:
         load.start()
+    loads[2].wait()
+    lane = lax.broadcasted_iota(jnp.int32, (8, LANES), 1)
+    for z in range(count_z):
+        tile = jnp.zeros((8, LANES), jnp.float32)
+        for i in range(part_rows // 8):
+            column = jnp.broadcast_to(tail[z, 8 * i:8 * i + 8, LANES - 1:], (8, LANES))
+            tile = jnp.where(lane == i, column, tile)
+        packed[z] = tile
 
     barrier = pltpu.get_barrier_semaphore()
 
@@ -122,8 +132,7 @@
     def edge_sends(do):
         for z in range(count_z):
             y = wrap(py + 1)
-            do(p_hbm.at[y * count_z + z, :, width - LANES:], left.at[mine],
-               edge_s.at[z], edge_r.at[pz], y, z, away=True)
+            do(packed.at[z], edge.at[pz], edge_s.at[z], edge_r.at[pz], y, z, away=True)
 
     def forward(k, do):
         c = cols(wrap(py + k))
@@ -148,13 +157,17 @@
             do(out.at[0, band(z), cols(y)], got_x.at[below], x_s.at[slot], x_r.at[below], y, z,
                gate=jnp.minimum(me, 1 - passed(pz, z)))
 
-    edge_sends(begin)
     for k in range(min(AHEAD, count_y)):
         pressure_sends(k, begin)
-    for load in loads:
+        if k == 0:
+            edge_sends(begin)
+    for z in range(count_z):
+        landed(edge.at[z], edge_r.at[z])
+        for i in range(part_rows // 8):
+            rows_at = z * part_rows + 8 * i
+            left[rows_at:rows_at + 8] = jnp.broadcast_to(edge[z, :, i:i + 1], (8, LANES))
+    for load in loads[:2]:
         load.wait()
-    for z in range(count_z):
-        landed(left.at[band(z)], edge_r.at[z])
 
     def before(tile, values):
         wide = jnp.concatenate([tile, values], 1)
@@ -282,8 +295,9 @@
         out_specs=(pl.BlockSpec(memory_space=pltpu.VMEM),) * 2,
         scratch_shapes=[
             vm(3, rows, across), vm(rows, across), vm(rows, across), vm(rows, across), vm(rows, across),
-            vm(rows, LANES), vm(rows, across), vm(rows, across),
-            vm(planes, *block), vm(planes, *block), dma(2),
+            vm(rows, LANES), vm(count_z, block[0], LANES), vm(count_z, 8, LANES), vm(count_z, 8, LANES),
+            vm(rows, across), vm(rows, across),
+            vm(planes, *block), vm(planes, *block), dma(3),
             dma(steps), dma(steps), dma(steps), dma(steps), dma(count_z), dma(count_z),
             dma(count_y), dma(count_y), dma(steps), dma(steps), dma(steps), dma(steps),
             dma(steps), dma(planes), dma(steps), dma(planes),

time: 111 us -> 113 us (1.018)
  Pallas kernels: 107 us -> 110 us
    pallas_call x1, Pallas kernels: 107 us -> 110 us  [on_device(): pl.pallas_call(functools.partial(kernel, count_y, count_z), out_shape=(ja...]
where the time goes in v4:
time: 113 us
  Pallas kernels  110 us (97%)
  local copies, waits for them, and re-layouts  2.64 us (2%)
    pallas_call x1, Pallas kernels, on_device(): pl.pallas_call(functools.partial(kernel, count_y, count_z), out_shape=(ja...  110 us
    unnamed x2, local copies, waits for them, and re-layouts  2.64 us

profile of v4, /device:TPU:1, one launch (start us, length us, event | category | flops | bytes accessed | tf_op | source)
XLA Modules:
  0.0 113.3 jit_solution(2965072318250415300)
XLA Ops:
  0.6 110.0 %project_all.1 = (f32[3,1,128,2048]{3,2,1,0:T(8,128)S(1)}, f32[32,32,256]{2,1,0:T(8,128)S(1)}) custom-call(f32[3,1,128,2048]{3,2,1,0:T(8,128)} %v_hbm.1, f32[1,128,2048]{2,1,0:T(8,128)} %f_hbm.1, f32[32,32,256]{2,1,0:T(8,128)} %p_hbm.1), custom_call_target="tpu_custom_call" | custom-call | tf_op jit(solution)/shard_map/project_all/pallas_call | solution.py:288
  110.7 1.7 %copy.7 = f32[3,1,128,2048]{3,2,1,0:T(8,128)} copy(f32[3,1,128,2048]{3,2,1,0:T(8,128)S(1)} %get-tuple-element.4) | data formatting | bytes 6291456
  112.3 1.0 copy.8

commit v5 on v3

--- a/solution.py
+++ b/solution.py
@@ -8,6 +8,7 @@
 from jax.sharding import PartitionSpec as P
 
 AHEAD = 2
+AHEAD_F = 1
 LANES = 128
 
 
@@ -115,6 +116,8 @@
 
             do(p_hbm.at[jnp.maximum(target - 1, 0)], halo.at[mine, cols(py)],
                halo_s.at[slot], halo_r.at[k * count_z + pz], y, z, gate=1 - passed(z, pz))
+
+    def fluid_sends(k, do):
         c = cols(wrap(ahead_y + k))
         do(f_hbm.at[0, :, c], f_low.at[:, c], f_s.at[k], f_r.at[k], ahead_y, ahead_z,
            gate=planes - 1 - me, away=True)
@@ -151,6 +154,8 @@
     edge_sends(begin)
     for k in range(min(AHEAD, count_y)):
         pressure_sends(k, begin)
+    for k in range(min(AHEAD_F, count_y)):
+        fluid_sends(k, begin)
     for load in loads:
         load.wait()
     for z in range(count_z):
@@ -164,6 +169,10 @@
         @pl.when(k + AHEAD < count_y)
         def _():
             pressure_sends(k + AHEAD, begin)
+
+        @pl.when(k + AHEAD_F < count_y)
+        def _():
+            fluid_sends(k + AHEAD_F, begin)
 
         y = wrap(py + k)
         c = cols(y)
@@ -254,6 +263,7 @@
 
     def finish(k, carry):
         pressure_sends(k, sent)
+        fluid_sends(k, sent)
         forward(k, sent)
         lend(k, sent)
         result_sends(k, sent)

time: 111 us -> 109 us (0.982)
    pallas_call x1, Pallas kernels: 107 us -> 106 us  [on_device(): pl.pallas_call(functools.partial(kernel, count_y, count_z), out_shape=(ja...]
where the time goes in v5:
time: 109 us
  Pallas kernels  106 us (97%)
  local copies, waits for them, and re-layouts  2.64 us (2%)
    pallas_call x1, Pallas kernels, on_device(): pl.pallas_call(functools.partial(kernel, count_y, count_z), out_shape=(ja...  106 us
    unnamed x2, local copies, waits for them, and re-layouts  2.64 us

profile of v5, /device:TPU:1, one launch (start us, length us, event | category | flops | bytes accessed | tf_op | source)
XLA Modules:
  0.0 109.0 jit_solution(5821878473185459627)
XLA Ops:
  0.6 105.7 %project_all.1 = (f32[3,1,128,2048]{3,2,1,0:T(8,128)S(1)}, f32[32,32,256]{2,1,0:T(8,128)S(1)}) custom-call(f32[3,1,128,2048]{3,2,1,0:T(8,128)} %v_hbm.1, f32[1,128,2048]{2,1,0:T(8,128)} %f_hbm.1, f32[32,32,256]{2,1,0:T(8,128)} %p_hbm.1), custom_call_target="tpu_custom_call" | custom-call | tf_op jit(solution)/shard_map/project_all/pallas_call | solution.py:285
  106.3 1.7 %copy.7 = f32[3,1,128,2048]{3,2,1,0:T(8,128)} copy(f32[3,1,128,2048]{3,2,1,0:T(8,128)S(1)} %get-tuple-element.4) | data formatting | bytes 6291456
  108.0 1.0 copy.8
